TPU v7x, 256 devices: a whole 4x4x8 slice. The times are simulated.
256 devices in a mesh: seq: 64 (over y, z, core), head: 4 (over x).
Axes of the slice: x: 4, y: 4, z: 8, core: 2. Of those that a mesh axis runs over, the one named last changes fastest.
Arguments:
- queries: bfloat16 [65536, 512], P('seq', 'head'), may hold values from -6 to 6
- keys: bfloat16 [65536, 512], P('seq', 'head'), may hold values from -6 to 6
- values: bfloat16 [65536, 512], P('seq', 'head'), may hold values from -6 to 6
- outputs: bfloat16 [65536, 512], P('seq', 'head'), may hold values from -6 to 6
- d_outputs: bfloat16 [65536, 512], P('seq', 'head'), may hold values from -6 to 6
- log_norm: float32 [8, 65536], P('head', 'seq'), may hold values from 4 to 5.5
- rand_owner: int32 [512, 3], P('seq'), may hold values from 0 to 63, all different within a row; in each aligned block of 8 rows (0 to 7, 8 to 15, ...) at most 2 rows name the same one
- rand_local: int32 [512, 3], P('seq'), may hold values from 0 to 7
- glob_blocks: int32 [2], replicated, may hold values from 0 to 511
Outputs:
- d_queries: bfloat16 [65536, 512], P('seq', 'head')
- d_keys: bfloat16 [65536, 512], P('seq', 'head')
- d_values: bfloat16 [65536, 512], P('seq', 'head')
Inputs may be any that keep to these rules, and one draw needn't show every extreme that they name: `rand_owner`: each row names 3 different seq indices; within the 8 rows of one seq index no value is named more than 2 times, a bound that some block reaches.
All inputs are finite; a program needn't handle non-finite values.
Results may differ from a plain program's by a relative error of at most 0.0085.
Values may be sent and summed in bfloat16 or wider, within the bound.
A program may use at most 128 MiB of HBM per device.

v0:
```python
import math
import jax
import jax.numpy as jnp
from jax import lax
from jax.sharding import PartitionSpec as P

BLOCK = 128


def extended(array, sides, width):
    for axis, dim in sides:
        size, length = (lax.axis_size(axis), array.shape[dim])
        up = [(i, (i + 1) % size) for i in range(size - 1)]
        down = [(j, i) for i, j in up]
        last = lax.slice_in_dim(array, length - width, length, axis=dim)
        leading = lax.slice_in_dim(array, 0, width, axis=dim)
        before = lax.ppermute(last, axis, up)
        after = lax.ppermute(leading, axis, down)
        array = jnp.concatenate([before, array, after], axis=dim)
    return array


def pair_terms(query_rows, grad_rows, norm_rows, delta_rows, key_rows, value_rows, factor):
    scores = (
        jnp.einsum("nqhd,nkhd->nhqk", query_rows, key_rows, preferred_element_type=jnp.float32)
        * factor
    )
    weights = jnp.exp(scores - norm_rows[..., None])
    grad_weights = jnp.einsum(
        "nqhd,nkhd->nhqk", grad_rows, value_rows, preferred_element_type=jnp.float32
    )
    grad_scores = weights * (grad_weights - delta_rows[..., None])
    weights_low = weights.astype(jnp.bfloat16)
    scores_low = grad_scores.astype(jnp.bfloat16)
    grad_query = (
        jnp.einsum("nhqk,nkhd->nqhd", scores_low, key_rows, preferred_element_type=jnp.float32)
        * factor
    )
    grad_key = (
        jnp.einsum("nhqk,nqhd->nkhd", scores_low, query_rows, preferred_element_type=jnp.float32)
        * factor
    )
    grad_value = jnp.einsum(
        "nhqk,nqhd->nkhd", weights_low, grad_rows, preferred_element_type=jnp.float32
    )
    return (grad_query, grad_key, grad_value)


def add_by_block(targets, block_ids, blocks):
    selector = (block_ids[:, None] == jnp.arange(blocks, dtype=jnp.int32)[None, :]).astype(
        jnp.bfloat16
    )
    flat_terms = targets.reshape(targets.shape[0], -1)
    high_part = flat_terms.astype(jnp.bfloat16)
    low_part = (flat_terms - high_part.astype(jnp.float32)).astype(jnp.bfloat16)
    summed = jnp.einsum("sn,sf->nf", selector, high_part, preferred_element_type=jnp.float32)
    summed = summed + jnp.einsum(
        "sn,sf->nf", selector, low_part, preferred_element_type=jnp.float32
    )
    return summed.reshape((blocks,) + targets.shape[1:])


def shards(
    queries, keys, values, outputs, d_outputs, log_norm, rand_owner, rand_local, glob_blocks
):
    tokens_here, features = queries.shape
    heads_here = log_norm.shape[0]
    head_size = features // heads_here
    blocks = tokens_here // BLOCK
    per_block = rand_owner.shape[1]
    factor = 1.0 / math.sqrt(head_size)
    owners = lax.axis_size("seq")
    seq_index = lax.axis_index("seq")
    block_shape = (blocks, BLOCK, heads_here, head_size)
    query_blocks = queries.reshape(block_shape)
    grad_blocks = d_outputs.reshape(block_shape)
    split_out = outputs.reshape(tokens_here, heads_here, head_size).astype(jnp.float32)
    split_grad = d_outputs.reshape(tokens_here, heads_here, head_size).astype(jnp.float32)
    delta_flat = jnp.sum(split_out * split_grad, axis=-1).T
    delta_blocks = delta_flat.reshape(heads_here, blocks, BLOCK).transpose(1, 0, 2)
    norm_blocks = log_norm.reshape(heads_here, blocks, BLOCK).transpose(1, 0, 2)
    d_queries = jnp.zeros(block_shape, jnp.float32)
    pad_shape = (blocks + 2,) + block_shape[1:]
    keys_grad_pad = jnp.zeros(pad_shape, jnp.float32)
    values_grad_pad = jnp.zeros(pad_shape, jnp.float32)
    padded = extended(jnp.stack([keys, values]), (("seq", 1),), BLOCK)
    keys_pad = padded[0].reshape(pad_shape)
    values_pad = padded[1].reshape(pad_shape)
    for offset in range(3):
        grad_query, grad_key, grad_value = pair_terms(
            query_blocks,
            grad_blocks,
            norm_blocks,
            delta_blocks,
            keys_pad[offset : offset + blocks],
            values_pad[offset : offset + blocks],
            factor,
        )
        d_queries = d_queries + grad_query
        keys_grad_pad = keys_grad_pad.at[offset : offset + blocks].add(grad_key)
        values_grad_pad = values_grad_pad.at[offset : offset + blocks].add(grad_value)
    outgoing_edges = jnp.stack(
        [
            jnp.concatenate([keys_grad_pad[0], keys_grad_pad[blocks + 1]], axis=0).reshape(
                2 * BLOCK, features
            ),
            jnp.concatenate([values_grad_pad[0], values_grad_pad[blocks + 1]], axis=0).reshape(
                2 * BLOCK, features
            ),
        ]
    )
    arrived = extended(outgoing_edges.astype(jnp.bfloat16), (("seq", 1),), BLOCK).astype(
        outgoing_edges.dtype
    )
    from_before = arrived[:, :BLOCK].reshape((2,) + block_shape[1:])
    from_after = arrived[:, 3 * BLOCK :].reshape((2,) + block_shape[1:])
    d_keys = (
        keys_grad_pad[1 : blocks + 1].at[0].add(from_before[0]).at[blocks - 1].add(from_after[0])
    )
    d_values = (
        values_grad_pad[1 : blocks + 1].at[0].add(from_before[1]).at[blocks - 1].add(from_after[1])
    )
    global_owner = glob_blocks // blocks
    global_local = glob_blocks % blocks
    owned_here = (global_owner == seq_index).astype(jnp.float32)
    key_table = keys.reshape(blocks, BLOCK, features)
    value_table = values.reshape(blocks, BLOCK, features)
    own_part = jnp.stack([key_table[global_local], value_table[global_local]], axis=1).astype(
        jnp.float32
    )
    own_part = own_part * owned_here[:, None, None, None]
    shared = lax.psum(own_part, "seq").astype(jnp.bfloat16)
    global_pieces = []
    for number in range(shared.shape[0]):
        key_rows = jnp.broadcast_to(shared[number, 0].reshape(block_shape[1:]), block_shape)
        value_rows = jnp.broadcast_to(shared[number, 1].reshape(block_shape[1:]), block_shape)
        grad_query, grad_key, grad_value = pair_terms(
            query_blocks, grad_blocks, norm_blocks, delta_blocks, key_rows, value_rows, factor
        )
        d_queries = d_queries + grad_query
        global_pieces.append(
            jnp.stack(
                [
                    jnp.sum(grad_key, axis=0).reshape(BLOCK, features),
                    jnp.sum(grad_value, axis=0).reshape(BLOCK, features),
                ]
            )
        )
    totals = lax.psum(jnp.stack(global_pieces), "seq")
    for number in range(shared.shape[0]):
        d_keys = d_keys.at[global_local[number]].add(
            owned_here[number] * totals[number, 0].reshape(block_shape[1:])
        )
        d_values = d_values.at[global_local[number]].add(
            owned_here[number] * totals[number, 1].reshape(block_shape[1:])
        )
    references = blocks * per_block
    capacity = max(2, (references + owners - 1) // owners)
    owner_flat = rand_owner.reshape(-1)
    local_flat = rand_local.reshape(-1)
    matches = (owner_flat[:, None] == jnp.arange(owners, dtype=jnp.int32)[None, :]).astype(
        jnp.int32
    )
    within = jnp.sum((jnp.cumsum(matches, axis=0) - 1) * matches, axis=1)
    slot_index = owner_flat * capacity + within
    requested = jnp.zeros((owners * capacity,), jnp.int32).at[slot_index].set(local_flat)
    wanted = lax.all_to_all(
        requested.reshape(owners, capacity), "seq", split_axis=0, concat_axis=0, tiled=True
    )
    wanted_flat = wanted.reshape(-1)
    outgoing = jnp.stack([key_table[wanted_flat], value_table[wanted_flat]], axis=1)
    fetched = lax.all_to_all(
        outgoing.reshape(owners, capacity, 2, BLOCK, features),
        "seq",
        split_axis=0,
        concat_axis=0,
        tiled=True,
    )
    picked = fetched.reshape(owners * capacity, 2, BLOCK, features)[slot_index]
    picked = picked.reshape((blocks, per_block, 2) + block_shape[1:])
    pieces = []
    for column in range(per_block):
        grad_query, grad_key, grad_value = pair_terms(
            query_blocks,
            grad_blocks,
            norm_blocks,
            delta_blocks,
            picked[:, column, 0],
            picked[:, column, 1],
            factor,
        )
        d_queries = d_queries + grad_query
        pieces.append(jnp.stack([grad_key, grad_value], axis=1))
    partials = jnp.stack(pieces, axis=1).reshape(references, 2, BLOCK, features)
    returned = (
        jnp.zeros((owners * capacity, 2, BLOCK, features), jnp.float32).at[slot_index].set(partials)
    )
    received = lax.all_to_all(
        returned.reshape(owners, capacity, 2, BLOCK, features).astype(jnp.bfloat16),
        "seq",
        split_axis=0,
        concat_axis=0,
        tiled=True,
    ).astype(jnp.float32)
    summed = add_by_block(
        received.reshape(owners * capacity, 2, BLOCK, features), wanted_flat, blocks
    )
    d_keys = d_keys + summed[:, 0].reshape(block_shape)
    d_values = d_values + summed[:, 1].reshape(block_shape)
    return (
        d_queries.reshape(tokens_here, features).astype(jnp.bfloat16),
        d_keys.reshape(tokens_here, features).astype(jnp.bfloat16),
        d_values.reshape(tokens_here, features).astype(jnp.bfloat16),
    )


def solution(mesh):
    placed = (
        P("seq", "head"),
        P("seq", "head"),
        P("seq", "head"),
        P("seq", "head"),
        P("seq", "head"),
        P("head", "seq"),
        P("seq", None),
        P("seq", None),
        P(),
    )
    return jax.shard_map(
        shards,
        mesh=mesh,
        in_specs=placed,
        out_specs=(P("seq", "head"), P("seq", "head"), P("seq", "head")),
        check_vma=False,
    )
```

profile of v0, /device:TPU:1, one launch (start us, length us, event | category | flops | bytes accessed | tf_op | source)
XLA Modules:
  0.0 938.5 jit_solution(7537119073880668998)
XLA Ops:
  10.9 22.2 %all_to_all.19 = s32[64,1,2]{2,1,0:T(1,128)S(1)} all-to-all(s32[64,1,2]{2,1,0:T(1,128)S(1)} %bitcast.340), channel_id=1, replica_groups=mesh['seq'=64,'head'=4] {'seq'}, dimensions={0} | all-to-all | bytes 1024 | tf_op jit(solution)/shard_map/all_to_all | solution.py:167
  34.5 3.1 gather_fusion.3
  37.6 3.0 gather_fusion.2
  40.6 7.5 pad_maximum_fusion
  48.1 5.9 all-to-all-start.1
  55.2 184.7 %all-to-all-done.1 = bf16[64,2,2,128,128]{4,3,1,2,0:T(8,128)(2,1)} async-done(((bf16[64,2,2,128,128]{4,3,1,2,0:T(8,128)(2,1)}), bf16[64,2,2,128,128]{4,3,1,2,0:T(8,128)(2,1)}, u32[]{:S(2)}, u32[]{:S(2)}) %all-to-all-start.1) | async-done | bytes 8388640 | tf_op jit(solution)/shard_map/all_to_all | solution.py:172
  239.8 10.3 %copy.256 = bf16[64,2,2,128,128]{4,3,2,1,0:T(8,128)(2,1)} copy(bf16[64,2,2,128,128]{4,3,1,2,0:T(8,128)(2,1)} %all-to-all-done.1) | data formatting | bytes 16777216 | tf_op jit(solution)/shard_map/all_to_all | solution.py:172
  250.2 5.4 gather_fusion.4
  265.2 3.5 copy.290
  268.7 7.9 broadcast_in_dim.17
  276.6 7.7 scatter_fusion
  284.2 9.2 convert_element_type.120
  293.4 6.3 all-to-all-start.2
  300.5 3.5 collective-permute-start
  307.2 409.5 %all-reduce.6 = bf16[2,2,128,128]{3,2,0,1:T(8,128)(2,1)S(1)} all-reduce(f32[2,2,128,128]{3,2,0,1:T(8,128)S(1)} %convert_multiply_fusion.1), channel_id=1, replica_groups=mesh['seq'=64,'head'=4] {'seq'}, use_global_device_ids=true, to_apply=%region_1.0 | all-reduce | flops 65536 | bytes 393216 | tf_op jit(solution)/shard_map/psum | solution.py:132
  730.7 2.1 convolution_bitcast_fusion.10
  748.2 3.6 collective-permute-start.2
  751.8 5.7 collective-permute-start.3
  761.9 133.5 %all-reduce.5.cloned.1.call-done = f32[2,2,128,128]{2,3,1,0:T(8,128)} async-done(((f32[2,2,128,128]{2,3,1,0:T(8,128)}), f32[2,2,128,128]{2,3,1,0:T(8,128)}) %all-reduce.5.cloned.1.call-update) | async-done | bytes 262160 | tf_op jit(solution)/shard_map/psum | solution.py:149
  895.4 2.3 slice_multiply_fusion
  897.7 2.1 fusion.76
  899.8 2.1 fusion.77
  906.6 13.3 %reshape_reshape.6 = bf16[128,32768]{1,0:T(8,128)(2,1)} reshape(bf16[64,2,2,128,128]{4,3,2,1,0:T(8,128)(2,1)} %all-to-all-done.2) | data formatting | bytes 16777216 | tf_op jit(solution)/shard_map/reshape;reshape | solution.py:53
  919.9 4.8 fusion.84
  (199 shorter events, 60.5 us)
Async XLA Ops:
  7.2 27.3 %copy-start = (bf16[1024,128]{1,0:T(8,128)(2,1)S(1)}, bf16[1024,128]{1,0:T(8,128)(2,1)}, u32[]{:S(2)}) copy-start(bf16[1024,128]{1,0:T(8,128)(2,1)} %param.39) | copy-start | bytes 786436
  48.1 6.0 copy-start.26
  48.1 6.2 copy-start.27
  48.1 6.4 copy-start.25
  48.1 191.7 %all-to-all-start.1 = ((bf16[64,2,2,128,128]{4,3,1,2,0:T(8,128)(2,1)}), bf16[64,2,2,128,128]{4,3,1,2,0:T(8,128)(2,1)}, u32[]{:S(2)}, u32[]{:S(2)}) async-start(bf16[64,2,2,128,128]{4,3,1,2,0:T(8,128)(2,1)} %pad_maximum_fusion), calls=%async_computation.1 | async-start | bytes 16777216 | tf_op jit(solution)/shard_map/all_to_all | solution.py:172
  250.2 7.3 copy-start.24
  293.4 12.5 %copy-start.29 = (s32[2]{0:T(128)S(1)}, s32[2]{0:T(128)}, u32[]{:S(2)}) copy-start(s32[2]{0:T(128)} %param.45) | copy-start | bytes 28
  293.4 613.1 %all-to-all-start.2 = ((bf16[64,2,2,128,128]{4,3,2,1,0:T(8,128)(2,1)}), bf16[64,2,2,128,128]{4,3,2,1,0:T(8,128)(2,1)}, u32[]{:S(2)}, u32[]{:S(2)}) async-start(bf16[64,2,2,128,128]{4,3,2,1,0:T(8,128)(2,1)} %bitcast.283), calls=%async_computation.2 | async-start | bytes 16777216 | tf_op jit(solution)/shard_map/all_to_all | solution.py:198
  299.8 595.6 %all-reduce.5.cloned.1.call-start = ((), (), s32[]{:S(2)}) async-start(), calls=%async_computation.3 | async-start | bytes 524288 | tf_op jit(solution)/shard_map/psum | solution.py:149
  300.5 437.4 %collective-permute-start = (bf16[2,128,128]{2,1,0:T(8,128)(2,1)}, bf16[2,128,128]{2,1,0:T(8,128)(2,1)}, u32[]{:S(2)}, u32[]{:S(2)}) collective-permute-start(bf16[2,128,128]{2,1,0:T(8,128)(2,1)} %get-tuple-element.192), channel_id=1, source_target_pairs={{0,4},{4,8},{8,12},{12,16},{16,20},{20,24},{24,28},{28,32},{32,36}... | collective-permute-start | bytes 196616 | tf_op jit(solution)/shard_map/ppermute | solution.py:17
  304.0 433.8 %collective-permute-start.1 = (bf16[2,128,128]{2,1,0:T(8,128)(2,1)}, bf16[2,128,128]{2,1,0:T(8,128)(2,1)}, u32[]{:S(2)}, u32[]{:S(2)}) collective-permute-start(bf16[2,128,128]{2,1,0:T(8,128)(2,1)} %get-tuple-element.193), channel_id=1, source_target_pairs={{4,0},{8,4},{12,8},{16,12},{20,16},{24,20},{28,24},{32,28},{36,32}... | collective-permute-start | bytes 196616 | tf_op jit(solution)/shard_map/ppermute | solution.py:18
  719.5 9.4 copy-start.28
  728.9 5.6 copy-start.21
  739.6 3.3 copy-start.23
  748.2 11.3 %collective-permute-start.2 = (bf16[2,128,128]{1,2,0:T(8,128)(2,1)S(1)}, bf16[2,128,128]{1,2,0:T(8,128)(2,1)S(1)}, u32[]{:S(2)}, u32[]{:S(2)}) collective-permute-start(bf16[2,128,128]{1,2,0:T(8,128)(2,1)S(1)} %get-tuple-element.201), channel_id=1, source_target_pairs={{0,4},{4,8},{8,12},{12,16},{16,20},{20,24},{24,28},{28,32},{32,36}... | collective-permute-start | bytes 196616 | tf_op jit(solution)/shard_map/ppermute | solution.py:17
  751.8 152.2 %copy-start.8 = (bf16[8,2,128,128]{3,2,1,0:T(8,128)(2,1)S(1)}, bf16[8,2,128,128]{3,2,1,0:T(8,128)(2,1)}, u32[]{:S(2)}) copy-start(bf16[8,2,128,128]{3,2,1,0:T(8,128)(2,1)} %copy-done.7) | copy-start | bytes 1572868
  751.8 7.7 collective-permute-start.3
  758.6 145.7 %copy-start.10 = (bf16[8,2,128,128]{3,2,1,0:T(8,128)(2,1)S(1)}, bf16[8,2,128,128]{3,2,1,0:T(8,128)(2,1)}, u32[]{:S(2)}) copy-start(bf16[8,2,128,128]{3,2,1,0:T(8,128)(2,1)} %copy-done.9) | copy-start | bytes 1572868
  895.4 9.2 copy-start.12
  895.4 9.5 %copy-start.15 = (f32[8,128,2,64]{1,3,2,0:T(8,128)S(1)}, f32[8,128,2,64]{1,3,2,0:T(8,128)}, u32[]{:S(2)}) copy-start(f32[8,128,2,64]{1,3,2,0:T(8,128)} %convolution_bitcast_fusion.9) | copy-start | bytes 1572868
  895.4 9.5 %copy-start.16 = (f32[8,128,2,64]{1,3,2,0:T(8,128)S(1)}, f32[8,128,2,64]{1,3,2,0:T(8,128)}, u32[]{:S(2)}) copy-start(f32[8,128,2,64]{1,3,2,0:T(8,128)} %convolution_bitcast_fusion.10) | copy-start | bytes 1572868
  895.4 9.5 %copy-start.17 = (f32[8,128,2,64]{1,3,2,0:T(8,128)S(1)}, f32[8,128,2,64]{1,3,2,0:T(8,128)}, u32[]{:S(2)}) copy-start(f32[8,128,2,64]{1,3,2,0:T(8,128)} %convolution_bitcast_fusion.12) | copy-start | bytes 1572868
  895.4 9.5 %copy-start.18 = (f32[8,128,2,64]{1,3,2,0:T(8,128)S(1)}, f32[8,128,2,64]{1,3,2,0:T(8,128)}, u32[]{:S(2)}) copy-start(f32[8,128,2,64]{1,3,2,0:T(8,128)} %convolution_bitcast_fusion.11) | copy-start | bytes 1572868
  919.9 5.8 copy-start.2
  (13 other events, 19.8 us)
Sparse Core Ops, SparseCore 0:
  721.2 174.0 all-reduce.4
where the time goes:
time: 940 us; the launch traced here: 939 us
  blocking collectives  432 us (46%)
  waiting for transfers between devices  318 us (34%)
  local copies, waits for them, and re-layouts  81.8 us (9%)
  other arithmetic  35.3 us (4%)
  starting transfers between devices  27 us (3%)
  matrix products  25.8 us (3%)
  between operations  18.7 us (2%)
    psum x1, blocking collectives, shards(): shared = lax.psum(own_part, 'seq').astype(jnp.bfloat16)  409 us
    all_to_all x1, waiting for transfers between devices, shards(): lax.all_to_all(outgoing.reshape(owners, capacity, 2, BLOCK, features), 's...  185 us
    psum x1, waiting for transfers between devices, shards(): totals = lax.psum(jnp.stack(global_pieces), 'seq')  133 us
    all_to_all x1, blocking collectives, shards(): lax.all_to_all(requested.reshape(owners, capacity), 'seq', split_axis=0,...  22.2 us
  transfers between devices with their start and end apart: 7, of which 2 were waited for; matrix products, arithmetic and copies ran while one was open for 5% of the time, Pallas kernels for 0%

commit v1 on v0

--- a/solution.py
+++ b/solution.py
@@ -146,7 +146,7 @@
                 ]
             )
         )
-    totals = lax.psum(jnp.stack(global_pieces), "seq")
+    totals = jnp.sum(lax.all_gather(jnp.stack(global_pieces), "seq"), axis=0)
     for number in range(shared.shape[0]):
         d_keys = d_keys.at[global_local[number]].add(
             owned_here[number] * totals[number, 0].reshape(block_shape[1:])

time: 940 us -> 853 us (0.907)
  blocking collectives: 432 us -> 246 us
  waiting for transfers between devices: 318 us -> 393 us
  starting transfers between devices: 27 us -> 41 us
  local copies, waits for them, and re-layouts: 81.8 us -> 92.7 us
    psum x1, blocking collectives: 409 us -> 246 us  [shards(): shared = lax.psum(own_part, 'seq').astype(jnp.bfloat16)]
    ppermute x2, waiting for transfers between devices: 0.01 us -> 156 us  [extended(): before = lax.ppermute(last, axis, up)]
    psum x1 -> x0, waiting for transfers between devices: 133 us -> none  [shards(): totals = lax.psum(jnp.stack(global_pieces), 'seq')]
    all_to_all x1, waiting for transfers between devices: 185 us -> 231 us  [shards(): lax.all_to_all(outgoing.reshape(owners, capacity, 2, BLOCK, features), 's...]
    all_to_all x1 -> x0, blocking collectives: 22.2 us -> none  [shards(): lax.all_to_all(requested.reshape(owners, capacity), 'seq', split_axis=0,...]
    all_to_all x0 -> x1, starting transfers between devices: none -> 13.2 us  [shards(): lax.all_to_all(requested.reshape(owners, capacity), 'seq', split_axis=0,...]
  transfers between devices with their start and end apart: 7 -> 8, of which waited for: 2 -> 4; matrix products, arithmetic and copies ran while one was open for 5% -> 13% of each run, Pallas kernels for 0% -> 0%
where the time goes in v1:
time: 853 us; the launch traced here: 851 us
  waiting for transfers between devices  393 us (46%)
  blocking collectives  246 us (29%)
  local copies, waits for them, and re-layouts  92.7 us (11%)
  starting transfers between devices  41 us (5%)
  other arithmetic  33.8 us (4%)
  matrix products  25.9 us (3%)
  between operations  19 us (2%)
    psum x1, blocking collectives, shards(): shared = lax.psum(own_part, 'seq').astype(jnp.bfloat16)  246 us
    all_to_all x1, waiting for transfers between devices, shards(): lax.all_to_all(outgoing.reshape(owners, capacity, 2, BLOCK, features), 's...  231 us
    ppermute x2, waiting for transfers between devices, extended(): before = lax.ppermute(last, axis, up)  156 us
  transfers between devices with their start and end apart: 8, of which 4 were waited for; matrix products, arithmetic and copies ran while one was open for 13% of the time, Pallas kernels for 0%

profile of v1, /device:TPU:1, one launch (start us, length us, event | category | flops | bytes accessed | tf_op | source)
XLA Modules:
  0.0 851.3 jit_solution(18232944805550063768)
XLA Ops:
  11.5 13.2 %all-to-all-start = ((s32[64,1,2]{2,1,0:T(1,128)}), s32[64,1,2]{2,1,0:T(1,128)S(1)}, u32[]{:S(2)}, u32[]{:S(2)}) async-start(s32[64,1,2]{2,1,0:T(1,128)} %bitcast.23), calls=%async_computation | async-start | bytes 65536 | tf_op jit(solution)/shard_map/all_to_all | solution.py:167
  29.1 245.9 %all-reduce.3 = bf16[2,2,128,128]{3,2,0,1:T(8,128)(2,1)S(1)} all-reduce(f32[2,2,128,128]{3,2,0,1:T(8,128)S(1)} %convert_multiply_fusion.1), channel_id=1, replica_groups=mesh['seq'=64,'head'=4] {'seq'}, use_global_device_ids=true, to_apply=%region_1.0 | all-reduce | flops 65536 | bytes 393216 | tf_op jit(solution)/shard_map/psum | solution.py:132
  280.9 3.0 gather_fusion.3
  284.0 3.0 gather_fusion.2
  287.0 7.5 pad_maximum_fusion
  294.5 10.9 %all-to-all-start.1 = ((bf16[64,2,2,128,128]{4,3,1,2,0:T(8,128)(2,1)}), bf16[64,2,2,128,128]{4,3,1,2,0:T(8,128)(2,1)}, u32[]{:S(2)}, u32[]{:S(2)}) async-start(bf16[64,2,2,128,128]{4,3,1,2,0:T(8,128)(2,1)} %pad_maximum_fusion), calls=%async_computation.1 | async-start | bytes 16777216 | tf_op jit(solution)/shard_map/all_to_all | solution.py:172
  309.6 230.8 %all-to-all-done.1 = bf16[64,2,2,128,128]{4,3,1,2,0:T(8,128)(2,1)} async-done(((bf16[64,2,2,128,128]{4,3,1,2,0:T(8,128)(2,1)}), bf16[64,2,2,128,128]{4,3,1,2,0:T(8,128)(2,1)}, u32[]{:S(2)}, u32[]{:S(2)}) %all-to-all-start.1) | async-done | bytes 8388640 | tf_op jit(solution)/shard_map/all_to_all | solution.py:172
  540.3 10.3 %copy.427 = bf16[64,2,2,128,128]{4,3,2,1,0:T(8,128)(2,1)} copy(bf16[64,2,2,128,128]{4,3,1,2,0:T(8,128)(2,1)} %all-to-all-done.1) | data formatting | bytes 16777216 | tf_op jit(solution)/shard_map/all_to_all | solution.py:172
  550.7 5.4 gather_fusion.4
  566.4 3.5 copy.464
  569.9 7.9 broadcast_in_dim.17
  577.8 7.7 scatter_fusion
  585.5 9.2 %convert_element_type.120 = bf16[128,2,128,128]{3,2,1,0:T(8,128)(2,1)} convert(f32[128,2,128,128]{3,2,1,0:T(8,128)} %scatter_fusion) | non-fusion elementwise | flops 4194304 | bytes 25165824 | tf_op jit(solution)/shard_map/convert_element_type | solution.py:199
  594.7 6.2 all-to-all-start.2
  601.6 3.5 collective-permute-start
  605.1 2.1 collective-permute-start.1
  617.1 2.1 convolution_bitcast_fusion.10
  624.5 156.2 %collective-permute-done = bf16[2,128,128]{2,1,0:T(8,128)(2,1)} collective-permute-done((bf16[2,128,128]{2,1,0:T(8,128)(2,1)}, bf16[2,128,128]{2,1,0:T(8,128)(2,1)}, u32[]{:S(2)}, u32[]{:S(2)}) %collective-permute-start) | collective-permute-done | bytes 65568 | tf_op jit(solution)/shard_map/ppermute | solution.py:17
  780.7 3.4 collective-permute-done.1
  801.8 2.8 collective-permute-start.3
  804.9 2.5 collective-permute-done.3
  810.1 6.6 reduce_sum.72
  820.3 13.4 %reshape_reshape.6 = bf16[128,32768]{1,0:T(8,128)(2,1)} reshape(bf16[64,2,2,128,128]{4,3,2,1,0:T(8,128)(2,1)} %all-to-all-done.2) | data formatting | bytes 16777216 | tf_op jit(solution)/shard_map/reshape;reshape | solution.py:53
  833.7 4.8 fusion.84
  (184 shorter events, 70.2 us)
Async XLA Ops:
  7.2 273.7 %copy-start = (bf16[1024,128]{1,0:T(8,128)(2,1)S(1)}, bf16[1024,128]{1,0:T(8,128)(2,1)}, u32[]{:S(2)}) copy-start(bf16[1024,128]{1,0:T(8,128)(2,1)} %param.39) | copy-start | bytes 786436
  11.5 268.0 %all-to-all-start = ((s32[64,1,2]{2,1,0:T(1,128)}), s32[64,1,2]{2,1,0:T(1,128)S(1)}, u32[]{:S(2)}, u32[]{:S(2)}) async-start(s32[64,1,2]{2,1,0:T(1,128)} %bitcast.23), calls=%async_computation | async-start | bytes 65536 | tf_op jit(solution)/shard_map/all_to_all | solution.py:167
  280.9 3.1 copy-start.1
  294.5 11.1 %copy-start.17 = (f32[2,1024]{1,0:T(2,128)S(1)}, f32[2,1024]{1,0:T(2,128)}, u32[]{:S(2)}) copy-start(f32[2,1024]{1,0:T(2,128)} %param.42) | copy-start | bytes 24580
  294.5 245.9 %all-to-all-start.1 = ((bf16[64,2,2,128,128]{4,3,1,2,0:T(8,128)(2,1)}), bf16[64,2,2,128,128]{4,3,1,2,0:T(8,128)(2,1)}, u32[]{:S(2)}, u32[]{:S(2)}) async-start(bf16[64,2,2,128,128]{4,3,1,2,0:T(8,128)(2,1)} %pad_maximum_fusion), calls=%async_computation.1 | async-start | bytes 16777216 | tf_op jit(solution)/shard_map/all_to_all | solution.py:172
  305.4 504.8 %all-gather.3.cloned.1.call-start = ((), (), s32[]{:S(2)}) async-start(), calls=%async_computation.3 | async-start | bytes 17039360 | tf_op jit(solution)/shard_map/all_gather | solution.py:149
  307.9 242.8 %copy-start.14 = (bf16[8,2,128,128]{3,2,1,0:T(8,128)(2,1)}, bf16[8,2,128,128]{3,2,1,0:T(8,128)(2,1)S(1)}, u32[]{:S(2)}) copy-start(bf16[8,2,128,128]{3,2,1,0:T(8,128)(2,1)S(1)} %fusion.27) | copy-start | bytes 1572868
  558.7 1.8 copy-start.5
  594.7 20.6 %copy-start.18 = (s32[4]{0:T(128)S(1)}, s32[4]{0:T(128)}, u32[]{:S(2)}) copy-start(s32[4]{0:T(128)} %constant.366.clone.1) | copy-start | bytes 52
  594.7 225.7 %all-to-all-start.2 = ((bf16[64,2,2,128,128]{4,3,2,1,0:T(8,128)(2,1)}), bf16[64,2,2,128,128]{4,3,2,1,0:T(8,128)(2,1)}, u32[]{:S(2)}, u32[]{:S(2)}) async-start(bf16[64,2,2,128,128]{4,3,2,1,0:T(8,128)(2,1)} %bitcast.284), calls=%async_computation.2 | async-start | bytes 16777216 | tf_op jit(solution)/shard_map/all_to_all | solution.py:198
  601.6 179.1 %collective-permute-start = (bf16[2,128,128]{2,1,0:T(8,128)(2,1)}, bf16[2,128,128]{2,1,0:T(8,128)(2,1)}, u32[]{:S(2)}, u32[]{:S(2)}) collective-permute-start(bf16[2,128,128]{2,1,0:T(8,128)(2,1)} %get-tuple-element.198), channel_id=1, source_target_pairs={{0,4},{4,8},{8,12},{12,16},{16,20},{20,24},{24,28},{28,32},{32,36}... | collective-permute-start | bytes 196616 | tf_op jit(solution)/shard_map/ppermute | solution.py:17
  605.1 179.0 %collective-permute-start.1 = (bf16[2,128,128]{2,1,0:T(8,128)(2,1)}, bf16[2,128,128]{2,1,0:T(8,128)(2,1)}, u32[]{:S(2)}, u32[]{:S(2)}) collective-permute-start(bf16[2,128,128]{2,1,0:T(8,128)(2,1)} %get-tuple-element.199), channel_id=1, source_target_pairs={{4,0},{8,4},{12,8},{16,12},{20,16},{24,20},{28,24},{32,28},{36,32}... | collective-permute-start | bytes 196616 | tf_op jit(solution)/shard_map/ppermute | solution.py:18
  619.7 1.1 copy-start.3
  796.2 1.4 copy-start.4
  797.2 1.4 copy-start.15
  799.4 8.1 copy-start.6
  799.5 8.4 copy-start.8
  799.6 8.6 %copy-start.10 = (bf16[8,2,128,128]{3,2,1,0:T(8,128)(2,1)S(1)}, bf16[8,2,128,128]{3,2,1,0:T(8,128)(2,1)}, u32[]{:S(2)}) copy-start(bf16[8,2,128,128]{3,2,1,0:T(8,128)(2,1)} %copy-done.9) | copy-start | bytes 1572868
  799.7 5.3 collective-permute-start.2
  801.7 6.7 copy-start.11
  801.7 6.7 copy-start.12
  801.7 6.7 copy-start.13
  801.8 5.7 collective-permute-start.3
  833.7 5.8 copy-start.2
  (3 other events, 2.8 us)
Sparse Core Ops, SparseCore 0:
  309.7 216.6 all-gather.2
